TPU v7x, 256 devices: a whole 4x4x8 slice. The times are simulated.
256 devices in a mesh: seq: 8 (over z_hi, x), exp: 32 (over z_lo, y, core).
Axes of the slice: x: 4, y: 4, z: 8 (z_hi: 2, z_lo: 4; z = z_hi * 4 + z_lo), core: 2. Of those that a mesh axis runs over, the one named last changes fastest.
Arguments:
- tokens: bfloat16 [8192, 1664], P('seq'), may hold values from -6 to 6
- out_grad: bfloat16 [8192, 1664], P('seq'), may hold values from -6 to 6
- slot_params: bfloat16 [1024, 1664], P('exp'), may hold values from -6 to 6
- first_mixing: float32 [64, 4, 4, 4], P('exp'), may hold values from -3 to 3
- first_blocks: bfloat16 [64, 4, 416, 2048], P('exp', None, None, 'seq'), may hold values from -0.15625 to 0.15625
- second_mixing: float32 [64, 4, 4, 4], P('exp'), may hold values from -3 to 3
- second_blocks: bfloat16 [64, 4, 2048, 416], P('exp', None, 'seq'), may hold values from -0.0625 to 0.0625
Outputs:
- grad_tokens: float32 [8192, 1664], P(('seq', 'exp'))
- grad_slots: float32 [1024, 1664], P('exp')
- grad_first_mixing: float32 [64, 4, 4, 4], P('exp')
- grad_first_blocks: bfloat16 [64, 4, 416, 2048], P('exp', None, None, 'seq')
- grad_second_mixing: float32 [64, 4, 4, 4], P('exp')
- grad_second_blocks: bfloat16 [64, 4, 2048, 416], P('exp', None, 'seq')
All inputs are finite; a program needn't handle non-finite values.
Results may differ from a plain program's by a relative error of at most 0.04.
Values may be sent and summed in bfloat16 or wider, within the bound.
No kernel may reach another device: no remote copies, remote signals or barrier semaphores. Data moves between devices by JAX's collectives and lax.ppermute only.
A program may use at most 128 MiB of HBM per device.

v0:
```python
import jax
import jax.numpy as jnp
from jax import lax
from jax.sharding import PartitionSpec as P

logit_gain = 64.0
norm_eps = 1e-06
gelu_coef = 0.7978845608028654
cubic_coef = 0.044715


def gelu_pair(preact):
    inner_arg = gelu_coef * (preact + cubic_coef * preact * preact * preact)
    tangent = jnp.tanh(inner_arg)
    output = 0.5 * preact * (1.0 + tangent)
    slopes = 0.5 * (1.0 + tangent) + 0.5 * preact * (1.0 - tangent * tangent) * gelu_coef * (
        1.0 + 3.0 * cubic_coef * preact * preact
    )
    return (output, slopes)


def mix_blocks(blocks, mixing):
    return jnp.einsum("sak,iab->sbik", blocks.astype(jnp.float32), mixing)


def expert_forward(slot_in, first_mixing, first_blocks, second_mixing, second_blocks):
    slots_here, model_width = slot_in.shape
    factors = first_mixing.shape[0]
    inner_width = model_width // factors
    hidden_block = first_blocks.shape[2]
    first_flat = (
        mix_blocks(slot_in.reshape(slots_here, factors, inner_width), first_mixing)
        .astype(jnp.bfloat16)
        .reshape(slots_here * factors, factors * inner_width)
    )
    preact = jnp.dot(
        first_flat,
        first_blocks.reshape(factors * inner_width, hidden_block),
        preferred_element_type=jnp.float32,
    ).reshape(slots_here, factors, hidden_block)
    activated, slopes = gelu_pair(preact)
    hidden = activated.astype(jnp.bfloat16)
    second_flat = (
        mix_blocks(hidden, second_mixing)
        .astype(jnp.bfloat16)
        .reshape(slots_here * factors, factors * hidden_block)
    )
    slot_out = jnp.dot(
        second_flat,
        second_blocks.reshape(factors * hidden_block, inner_width),
        preferred_element_type=jnp.float32,
    ).reshape(slots_here, model_width)
    return (slot_out, first_flat, hidden, slopes, second_flat)


def expert_backward(
    slot_in,
    grad_out,
    first_flat,
    hidden,
    slopes,
    second_flat,
    first_mixing,
    first_blocks,
    second_mixing,
    second_blocks,
):
    slots_here, model_width = slot_in.shape
    factors = first_mixing.shape[0]
    inner_width = model_width // factors
    hidden_block = first_blocks.shape[2]
    first_matrix = first_blocks.reshape(factors * inner_width, hidden_block)
    second_matrix = second_blocks.reshape(factors * hidden_block, inner_width)
    grad_rows = grad_out.reshape(slots_here * factors, inner_width)
    grad_second_in = jnp.dot(
        grad_rows, second_matrix.T, preferred_element_type=jnp.float32
    ).reshape(slots_here, factors, factors, hidden_block)
    grad_second_blocks = (
        jnp.dot(second_flat.T, grad_rows, preferred_element_type=jnp.float32)
        .astype(jnp.bfloat16)
        .reshape(factors, hidden_block, inner_width)
    )
    grad_second_mixing = jnp.einsum("sak,sbik->iab", hidden.astype(jnp.float32), grad_second_in)
    grad_hidden = jnp.einsum("iab,sbik->sak", second_mixing, grad_second_in)
    grad_preact = (
        (grad_hidden * slopes).astype(jnp.bfloat16).reshape(slots_here * factors, hidden_block)
    )
    grad_first_in = jnp.dot(
        grad_preact, first_matrix.T, preferred_element_type=jnp.float32
    ).reshape(slots_here, factors, factors, inner_width)
    grad_first_blocks = (
        jnp.dot(first_flat.T, grad_preact, preferred_element_type=jnp.float32)
        .astype(jnp.bfloat16)
        .reshape(factors, inner_width, hidden_block)
    )
    slot_split = slot_in.reshape(slots_here, factors, inner_width).astype(jnp.float32)
    grad_first_mixing = jnp.einsum("sad,sbid->iab", slot_split, grad_first_in)
    grad_slot = jnp.einsum("iab,sbid->sad", first_mixing, grad_first_in).reshape(
        slots_here, model_width
    )
    return (grad_slot, grad_first_mixing, grad_first_blocks, grad_second_mixing, grad_second_blocks)


def token_total(partial_sums):
    return lax.psum(partial_sums, "exp")


def slot_total(first_part, second_part):
    return lax.psum((first_part, second_part), "seq")


def unit_grad(unit_rows, unit_grad_rows, norms):
    return (
        unit_grad_rows - unit_rows * jnp.sum(unit_rows * unit_grad_rows, axis=1, keepdims=True)
    ) / norms


def local(tokens, out_grad, slot_params, first_mixing, first_blocks, second_mixing, second_blocks):
    token_values = tokens.astype(jnp.float32)
    token_norm = jnp.sqrt(jnp.sum(token_values * token_values, axis=1, keepdims=True) + norm_eps)
    token_unit = token_values / token_norm
    token_unit_b = token_unit.astype(jnp.bfloat16)
    slot_values = slot_params.astype(jnp.float32)
    slot_norm = jnp.sqrt(jnp.sum(slot_values * slot_values, axis=1, keepdims=True) + norm_eps)
    slot_unit = slot_values / slot_norm
    slot_unit_b = slot_unit.astype(jnp.bfloat16)
    logits = logit_gain * jnp.einsum(
        "sd,td->st", slot_unit_b, token_unit_b, preferred_element_type=jnp.float32
    )
    weights = jnp.exp(logits)
    input_part = jnp.dot(weights.astype(jnp.bfloat16), tokens, preferred_element_type=jnp.float32)
    combine_total = token_total(jnp.sum(weights, axis=0))
    input_sum, dispatch_total = slot_total(input_part, jnp.sum(weights, axis=1))
    slot_inputs = input_sum / dispatch_total[:, None]
    slot_inputs_b = slot_inputs.astype(jnp.bfloat16)
    dispatch = weights / dispatch_total[:, None]
    combine = weights / combine_total[None, :]
    grad_out_part = jnp.dot(
        combine.astype(jnp.bfloat16), out_grad, preferred_element_type=jnp.float32
    )
    experts_here = first_mixing.shape[0]
    model_width = tokens.shape[1]
    slots_each = slot_inputs_b.shape[0] // experts_here
    grouped = slot_inputs_b.reshape(experts_here, slots_each, model_width)
    slot_out_part, first_flat, hidden, slopes, second_flat = jax.vmap(expert_forward)(
        grouped, first_mixing, first_blocks, second_mixing, second_blocks
    )
    slot_out_sum, slot_grad_sum = slot_total(
        slot_out_part.reshape(experts_here * slots_each, model_width), grad_out_part
    )
    slot_out_b = slot_out_sum.astype(jnp.bfloat16)
    slot_grad_b = slot_grad_sum.astype(jnp.bfloat16)
    combine_grad = jnp.einsum("sd,td->st", slot_out_b, out_grad, preferred_element_type=jnp.float32)
    combine_dot = token_total(jnp.sum(combine * combine_grad, axis=0))
    expert_results = jax.vmap(expert_backward)(
        grouped,
        slot_grad_b.reshape(experts_here, slots_each, model_width),
        first_flat,
        hidden,
        slopes,
        second_flat,
        first_mixing,
        first_blocks,
        second_mixing,
        second_blocks,
    )
    input_grad_part, first_mix_part, first_blocks_grad, second_mix_part, second_blocks_grad = (
        expert_results
    )
    input_grad, mixing_grads = slot_total(
        input_grad_part.reshape(experts_here * slots_each, model_width),
        jnp.stack([first_mix_part, second_mix_part]),
    )
    input_grad_b = input_grad.astype(jnp.bfloat16)
    dispatch_dot = jnp.sum(slot_inputs * input_grad, axis=1)
    dispatch_grad = jnp.einsum(
        "sd,td->st", input_grad_b, tokens, preferred_element_type=jnp.float32
    )
    logit_grad = combine * (combine_grad - combine_dot[None, :]) + dispatch * (
        dispatch_grad - dispatch_dot[:, None]
    )
    logit_grad_b = (logit_gain * logit_grad).astype(jnp.bfloat16)
    slot_unit_grad = lax.psum(
        jnp.dot(logit_grad_b, token_unit_b, preferred_element_type=jnp.float32), "seq"
    )
    grad_slots = unit_grad(slot_unit, slot_unit_grad, slot_norm)
    row_count = tokens.shape[0] // lax.axis_size("exp")
    grad_all, out_all, unit_all = (
        lax.all_gather(input_grad_b, "exp", axis=0, tiled=True),
        lax.all_gather(slot_out_b, "exp", axis=0, tiled=True),
        lax.all_gather(slot_unit_b, "exp", axis=0, tiled=True),
    )
    dispatch_all, dot_all = (
        lax.all_gather(dispatch_total, "exp", axis=0, tiled=True),
        lax.all_gather(dispatch_dot, "exp", axis=0, tiled=True),
    )
    first_row = lax.axis_index("exp") * row_count
    own_tokens = lax.dynamic_slice_in_dim(tokens, first_row, row_count, 0)
    own_grad = lax.dynamic_slice_in_dim(out_grad, first_row, row_count, 0)
    own_unit = lax.dynamic_slice_in_dim(token_unit, first_row, row_count, 0)
    own_unit_b = lax.dynamic_slice_in_dim(token_unit_b, first_row, row_count, 0)
    own_norm = lax.dynamic_slice_in_dim(token_norm, first_row, row_count, 0)
    own_total = lax.dynamic_slice_in_dim(combine_total, first_row, row_count, 0)
    own_dot = lax.dynamic_slice_in_dim(combine_dot, first_row, row_count, 0)
    own_weights = jnp.exp(
        logit_gain * jnp.dot(own_unit_b, unit_all.T, preferred_element_type=jnp.float32)
    )
    own_dispatch = own_weights / dispatch_all[None, :]
    own_combine = own_weights / own_total[:, None]
    own_combine_grad = jnp.dot(own_grad, out_all.T, preferred_element_type=jnp.float32)
    own_dispatch_grad = jnp.dot(own_tokens, grad_all.T, preferred_element_type=jnp.float32)
    own_logit = own_combine * (own_combine_grad - own_dot[:, None]) + own_dispatch * (
        own_dispatch_grad - dot_all[None, :]
    )
    own_logit_b = (logit_gain * own_logit).astype(jnp.bfloat16)
    direct = jnp.dot(
        own_dispatch.astype(jnp.bfloat16), grad_all, preferred_element_type=jnp.float32
    )
    through = jnp.dot(own_logit_b, unit_all, preferred_element_type=jnp.float32)
    grad_tokens = direct + unit_grad(own_unit, through, own_norm)
    return (
        grad_tokens,
        grad_slots,
        mixing_grads[0],
        first_blocks_grad,
        mixing_grads[1],
        second_blocks_grad,
    )


def solution(mesh):
    placed = (
        P("seq", None),
        P("seq", None),
        P("exp", None),
        P("exp", None, None, None),
        P("exp", None, None, "seq"),
        P("exp", None, None, None),
        P("exp", None, "seq", None),
    )
    return jax.shard_map(
        local,
        mesh=mesh,
        in_specs=placed,
        out_specs=(
            P(("seq", "exp"), None),
            P("exp", None),
            P("exp", None, None, None),
            P("exp", None, None, "seq"),
            P("exp", None, None, None),
            P("exp", None, "seq", None),
        ),
        check_vma=False,
    )
```

profile of v0, /device:TPU:1, one launch (start us, length us, event | category | flops | bytes accessed | tf_op | source)
XLA Modules:
  0.0 651.7 jit_solution(12688127571988477652)
XLA Ops:
  8.1 2.9 fusion
  11.2 5.0 convert_divide_fusion
  17.6 3.9 fusion.57
  23.0 71.5 %psum.64 = f32[1024]{0:T(1024)S(1)} all-reduce(f32[1024]{0:T(1024)S(1)} %get-tuple-element.19), channel_id=1, replica_groups=mesh['seq'=8,'exp'=32] {'exp'}, use_global_device_ids=true, to_apply=%region_5.0 | all-reduce | flops 1024 | bytes 8192 | tf_op jit(solution)/shard_map/psum | solution.py:105
  96.5 50.3 %all-reduce.16 = (bf16[32,1664]{1,0:T(8,128)(2,1)}, f32[32]{0:T(128)}) all-reduce(f32[32,1664]{1,0:T(8,128)} %fusion.41, f32[32]{0:T(128)} %get-tuple-element.18), channel_id=1, replica_groups=mesh['seq'=8,'exp'=32] {'seq'}, use_global_device_ids=true, to_apply=%region_6.0 | all-reduce | flops 53280 | bytes 319744 | tf_op jit(solution)/shard_map/psum | solution.py:109
  166.3 2.3 reshape.85
  168.6 2.7 fusion.67
  180.2 2.9 fusion.68
  183.0 2.5 reshape.89
  185.6 2.2 convolution_bitcast_fusion.2
  193.6 2.9 fusion.69
  198.3 2.2 convolution_bitcast_fusion
  203.7 46.9 %all-reduce.17 = (bf16[32,1664]{1,0:T(8,128)(2,1)}, f32[2,2,4,4,4]{4,3,2,1,0:T(4,128)}) all-reduce(f32[32,1664]{1,0:T(8,128)} %reshape.92, f32[2,2,4,4,4]{4,3,2,1,0:T(4,128)} %pad_maximum_fusion), channel_id=1, replica_groups=mesh['seq'=8,'exp'=32] {'seq'}, use_global_device_ids=true, to_apply=%region_9.0 | all-reduce | flops 53504 | bytes 321536 | tf_op jit(solution)/shard_map/psum | solution.py:109
  250.7 3.2 multiply_reduce_fusion.3
  253.9 51.0 %all-reduce.13.cloned.1.call-done = f32[32,1664]{1,0:T(8,128)} async-done(((f32[32,1664]{1,0:T(8,128)}), f32[32,1664]{1,0:T(8,128)}) %all-reduce.13.cloned.1.call-update) | async-done | bytes 213008 | tf_op jit(solution)/shard_map/psum | solution.py:109
  307.3 132.5 %all-reduce.2 = (f32[1024]{0:T(1024)}, f32[1024]{0:T(1024)}, f32[1024]{0:T(1024)S(1)}) all-reduce(f32[1024]{0:T(1024)} %get-tuple-element.34, f32[1024]{0:T(1024)S(1)} %dynamic-update-slice.1, f32[1024]{0:T(1024)S(1)} %copy-done.14), channel_id=1, replica_groups=mesh['seq'=8,'exp'=32] {'exp'}, use_global_device_ids=true, to_apply=%region_11.0 | all-reduce | flops 3072 | bytes 24576 | tf_op jit(solution)/shard_map/psum | solution.py:105
  439.8 5.5 fusion.16
  454.7 89.4 %all-reduce.15.cloned.1.call-done = f32[32,1664]{1,0:T(8,128)} async-done(((f32[32,1664]{1,0:T(8,128)}), f32[32,1664]{1,0:T(8,128)}) %all-reduce.15.cloned.1.call-update) | async-done | bytes 213008 | tf_op jit(solution)/shard_map/psum | solution.py:183
  547.0 3.2 fusion.12
  550.2 22.4 %all-gather.8.cloned.1.call-done = bf16[1024,1664]{1,0:T(8,128)(2,1)} async-done(((bf16[32,1664]{1,0:T(8,128)(2,1)}), bf16[1024,1664]{1,0:T(8,128)(2,1)}) %all-gather.8.cloned.1.call-update) | async-done | bytes 3407888 | tf_op jit(solution)/shard_map/all_gather | solution.py:190
  572.6 3.7 fusion.10
  576.3 59.0 %all-gather.6.cloned.1.call-done = bf16[1024,1664]{1,0:T(8,128)(2,1)} async-done(((bf16[32,1664]{1,0:T(8,128)(2,1)}), bf16[1024,1664]{1,0:T(8,128)(2,1)}) %all-gather.6.cloned.1.call-update) | async-done | bytes 3407888 | tf_op jit(solution)/shard_map/all_gather | solution.py:189
  635.3 5.5 multiply_reduce_fusion.1
  640.8 3.5 convolution_add_fusion
  (99 shorter events, 58.4 us)
Async XLA Ops:
  8.0 87.1 %copy-start = (bf16[1024,1664]{1,0:T(8,128)(2,1)S(1)}, bf16[1024,1664]{1,0:T(8,128)(2,1)}, u32[]{:S(2)}) copy-start(bf16[1024,1664]{1,0:T(8,128)(2,1)} %param.8) | copy-start | bytes 10223620
  8.0 152.4 %all-reduce.11.cloned.1.call-start = ((), (), s32[]{:S(2)}) async-start(), calls=%async_computation.1 | async-start | bytes 425984 | tf_op jit(solution)/shard_map/psum | solution.py:109
  8.1 3.1 copy-start.1
  11.2 5.0 copy-start.13
  11.2 5.0 copy-start.5
  17.6 3.9 copy-start.2
  23.0 282.0 %all-reduce.13.cloned.1.call-start = ((), (), s32[]{:S(2)}) async-start(), calls=%async_computation.2 | async-start | bytes 425984 | tf_op jit(solution)/shard_map/psum | solution.py:109
  96.5 59.4 %copy-start.9 = (f32[2,4,4,4]{3,2,1,0:T(4,128)S(1)}, f32[2,4,4,4]{3,2,1,0:T(4,128)}, u32[]{:S(2)}) copy-start(f32[2,4,4,4]{3,2,1,0:T(4,128)} %param.10) | copy-start | bytes 1540
  148.5 2.9 copy-start.7
  150.2 1.2 copy-start.3
  165.2 7.6 %copy-start.15 = (f32[2,4,4,4]{3,2,1,0:T(4,128)S(1)}, f32[2,4,4,4]{3,2,1,0:T(4,128)}, u32[]{:S(2)}) copy-start(f32[2,4,4,4]{3,2,1,0:T(4,128)} %param.12) | copy-start | bytes 1540
  202.3 341.8 %all-reduce.15.cloned.1.call-start = ((), (), s32[]{:S(2)}) async-start(), calls=%async_computation.5 | async-start | bytes 425984 | tf_op jit(solution)/shard_map/psum | solution.py:183
  203.7 101.2 %copy-start.18 = (f32[32]{0:T(128)S(1)}, f32[32]{0:T(128)}, u32[]{:S(2)}) copy-start(f32[32]{0:T(128)} %get-tuple-element.26) | copy-start | bytes 388
  203.7 103.6 %copy-start.14 = (f32[1024]{0:T(1024)S(1)}, f32[1024]{0:T(1024)}, u32[]{:S(2)}) copy-start(f32[1024]{0:T(1024)} %dynamic-update-slice) | copy-start | bytes 12292
  203.7 236.1 %copy-start.11 = (f32[1024]{0:T(1024)S(1)}, f32[1024]{0:T(1024)}, u32[]{:S(2)}) copy-start(f32[1024]{0:T(1024)} %copy-done.10) | copy-start | bytes 12292
  445.3 101.7 %all-gather.4.cloned.1.call-start = ((), (), s32[]{:S(2)}) async-start(), calls=%async_computation | async-start | bytes 3514368 | tf_op jit(solution)/shard_map/all_gather | solution.py:191
  445.9 126.6 %all-gather.8.cloned.1.call-start = ((), (), s32[]{:S(2)}) async-start(), calls=%async_computation.4 | async-start | bytes 3514368 | tf_op jit(solution)/shard_map/all_gather | solution.py:190
  446.5 188.8 %all-gather.6.cloned.1.call-start = ((), (), s32[]{:S(2)}) async-start(), calls=%async_computation.3 | async-start | bytes 3514368 | tf_op jit(solution)/shard_map/all_gather | solution.py:189
  447.1 3.9 copy-start.12
  447.1 4.5 copy-start.4
  447.1 4.5 copy-start.8
  448.0 96.1 %copy-start.6 = (bf16[32,1664]{1,0:T(8,128)(2,1)S(1)}, bf16[32,1664]{1,0:T(8,128)(2,1)}, u32[]{:S(2)}) copy-start(bf16[32,1664]{1,0:T(8,128)(2,1)} %param.9) | copy-start | bytes 319492
  448.0 96.1 %copy-start.17 = (f32[32]{0:T(128)S(1)}, f32[32]{0:T(128)}, u32[]{:S(2)}) copy-start(f32[32]{0:T(128)} %copy-done.16) | copy-start | bytes 388
  547.0 88.3 %copy-start.19 = (f32[1024]{0:T(1024)S(1)}, f32[1024]{0:T(1024)}, u32[]{:S(2)}) copy-start(f32[1024]{0:T(1024)} %get-tuple-element.21) | copy-start | bytes 12292
  (3 other events, 1.7 us)
Sparse Core Ops, SparseCore 0:
  23.1 102.7 all-reduce.10
  202.4 102.4 all-reduce.12
  445.5 98.6 all-reduce.14
Sparse Core Ops, SparseCore 1:
  447.7 62.2 all-gather.3
  511.8 60.7 all-gather.7
  574.3 61.0 all-gather.5
where the time goes:
time: 653 us; the launch traced here: 652 us
  blocking collectives  301 us (46%)
  waiting for transfers between devices  223 us (34%)
  matrix products  55.9 us (9%)
  local copies, waits for them, and re-layouts  38.1 us (6%)
  other arithmetic  16.5 us (3%)
  between operations  16.3 us (2%)
    psum x2, blocking collectives, token_total(): return lax.psum(partial_sums, 'exp')  204 us
    psum x2, blocking collectives, slot_total(): return lax.psum((first_part, second_part), 'seq')  97.3 us
    psum x1, waiting for transfers between devices, local(): lax.psum(jnp.dot(logit_grad_b, token_unit_b, preferred_element_type=jnp.f...  89.4 us
    all_gather x1, waiting for transfers between devices, local(): lax.all_gather(input_grad_b, 'exp', axis=0, tiled=True)  59 us
    psum x2, waiting for transfers between devices, slot_total(): return lax.psum((first_part, second_part), 'seq')  51 us
    all_gather x1, waiting for transfers between devices, local(): lax.all_gather(slot_out_b, 'exp', axis=0, tiled=True)  22.4 us
  transfers between devices with their start and end apart: 6, of which 4 were waited for; matrix products, arithmetic and copies ran while one was open for 5% of the time, Pallas kernels for 0%

commit v1 on v0

--- a/solution.py
+++ b/solution.py
@@ -186,7 +186,15 @@
     grad_slots = unit_grad(slot_unit, slot_unit_grad, slot_norm)
     row_count = tokens.shape[0] // lax.axis_size("exp")
     grad_all, out_all, unit_all = (
-        lax.all_gather(input_grad_b, "exp", axis=0, tiled=True),
+        jnp.concatenate(
+            lax.all_to_all(
+                jnp.stack([input_grad_b for _ in range(lax.axis_size("exp"))], 0),
+                axis_name="exp",
+                split_axis=0,
+                concat_axis=0,
+            ),
+            axis=0,
+        ),
         lax.all_gather(slot_out_b, "exp", axis=0, tiled=True),
         lax.all_gather(slot_unit_b, "exp", axis=0, tiled=True),
     )

time: 653 us -> 633 us (0.969)
  waiting for transfers between devices: 223 us -> 189 us
  starting transfers between devices: 0.25 us -> 10.9 us
    all_gather x1 -> x0, waiting for transfers between devices: 59 us -> none  [local(): lax.all_gather(input_grad_b, 'exp', axis=0, tiled=True)]
    psum x1, waiting for transfers between devices: 89.4 us -> 102 us  [local(): lax.psum(jnp.dot(logit_grad_b, token_unit_b, preferred_element_type=jnp.f...]
    all_gather x1, waiting for transfers between devices: 22.4 us -> 34.3 us  [local(): lax.all_gather(slot_out_b, 'exp', axis=0, tiled=True)]
    all_to_all x0 -> x1, starting transfers between devices: none -> 10.7 us  [local(): lax.all_to_all(jnp.stack([input_grad_b for _ in range(lax.axis_size('exp'...]
  transfers between devices with their start and end apart: 6 -> 6, of which waited for: 4 -> 3; matrix products, arithmetic and copies ran while one was open for 5% -> 6% of each run, Pallas kernels for 0% -> 0%
where the time goes in v1:
time: 633 us; the launch traced here: 631 us
  blocking collectives  300 us (47%)
  waiting for transfers between devices  189 us (30%)
  matrix products  56.8 us (9%)
  local copies, waits for them, and re-layouts  41.6 us (7%)
  other arithmetic  16.5 us (3%)
  between operations  16 us (3%)
  starting transfers between devices  10.9 us (2%)
    psum x2, blocking collectives, token_total(): return lax.psum(partial_sums, 'exp')  204 us
    psum x1, waiting for transfers between devices, local(): lax.psum(jnp.dot(logit_grad_b, token_unit_b, preferred_element_type=jnp.f...  102 us
    psum x2, blocking collectives, slot_total(): return lax.psum((first_part, second_part), 'seq')  96.3 us
    psum x2, waiting for transfers between devices, slot_total(): return lax.psum((first_part, second_part), 'seq')  51.7 us
    all_gather x1, waiting for transfers between devices, local(): lax.all_gather(slot_out_b, 'exp', axis=0, tiled=True)  34.3 us
  transfers between devices with their start and end apart: 6, of which 3 were waited for; matrix products, arithmetic and copies ran while one was open for 6% of the time, Pallas kernels for 0%

profile of v1, /device:TPU:1, one launch (start us, length us, event | category | flops | bytes accessed | tf_op | source)
XLA Modules:
  0.0 631.2 jit_solution(11375840291696572850)
XLA Ops:
  8.1 2.9 fusion
  11.2 5.0 convert_divide_fusion
  17.5 3.9 fusion.57
  22.9 71.5 %psum.64 = f32[1024]{0:T(1024)S(1)} all-reduce(f32[1024]{0:T(1024)S(1)} %get-tuple-element.19), channel_id=1, replica_groups=mesh['seq'=8,'exp'=32] {'exp'}, use_global_device_ids=true, to_apply=%region_5.0 | all-reduce | flops 1024 | bytes 8192 | tf_op jit(solution)/shard_map/psum | solution.py:105
  96.4 50.6 %all-reduce.16 = (bf16[32,1664]{1,0:T(8,128)(2,1)}, f32[32]{0:T(128)}) all-reduce(f32[32,1664]{1,0:T(8,128)} %fusion.41, f32[32]{0:T(128)} %get-tuple-element.18), channel_id=1, replica_groups=mesh['seq'=8,'exp'=32] {'seq'}, use_global_device_ids=true, to_apply=%region_6.0 | all-reduce | flops 53280 | bytes 319744 | tf_op jit(solution)/shard_map/psum | solution.py:109
  166.5 2.3 reshape.90
  168.8 2.7 fusion.67
  180.4 2.9 fusion.68
  183.3 2.5 reshape.94
  193.8 2.9 fusion.69
  204.0 45.7 %all-reduce.17 = (bf16[32,1664]{1,0:T(8,128)(2,1)}, f32[2,2,4,4,4]{4,3,2,1,0:T(4,128)}) all-reduce(f32[32,1664]{1,0:T(8,128)} %reshape.98, f32[2,2,4,4,4]{4,3,2,1,0:T(4,128)} %pad_maximum_fusion), channel_id=1, replica_groups=mesh['seq'=8,'exp'=32] {'seq'}, use_global_device_ids=true, to_apply=%region_9.0 | all-reduce | flops 53504 | bytes 321536 | tf_op jit(solution)/shard_map/psum | solution.py:109
  249.6 3.3 multiply_reduce_fusion.3
  252.9 51.7 %all-reduce.13.cloned.1.call-done = f32[32,1664]{1,0:T(8,128)} async-done(((f32[32,1664]{1,0:T(8,128)}), f32[32,1664]{1,0:T(8,128)}) %all-reduce.13.cloned.1.call-update) | async-done | bytes 213008 | tf_op jit(solution)/shard_map/psum | solution.py:109
  307.0 132.5 %all-reduce.2 = (f32[1024]{0:T(1024)}, f32[1024]{0:T(1024)}, f32[1024]{0:T(1024)S(1)}) all-reduce(f32[1024]{0:T(1024)} %get-tuple-element.34, f32[1024]{0:T(1024)S(1)} %dynamic-update-slice.1, f32[1024]{0:T(1024)S(1)} %copy-done.12), channel_id=1, replica_groups=mesh['seq'=8,'exp'=32] {'exp'}, use_global_device_ids=true, to_apply=%region_11.0 | all-reduce | flops 3072 | bytes 24576 | tf_op jit(solution)/shard_map/psum | solution.py:105
  439.5 5.5 fusion.16
  446.2 2.9 stack.8
  449.0 10.7 %all-to-all-start = ((bf16[32,32,1664]{2,1,0:T(8,128)(2,1)}), bf16[32,32,1664]{2,1,0:T(8,128)(2,1)}, u32[]{:S(2)}, u32[]{:S(2)}) async-start(bf16[32,32,1664]{2,1,0:T(8,128)(2,1)} %stack.8), calls=%async_computation | async-start | bytes 6815744 | tf_op jit(solution)/shard_map/all_to_all | solution.py:190
  464.9 2.7 convolution_convert_fusion
  468.9 102.1 %all-reduce.15.cloned.1.call-done = f32[32,1664]{1,0:T(8,128)} async-done(((f32[32,1664]{1,0:T(8,128)}), f32[32,1664]{1,0:T(8,128)}) %all-reduce.15.cloned.1.call-update) | async-done | bytes 213008 | tf_op jit(solution)/shard_map/psum | solution.py:183
  573.9 3.1 fusion.12
  577.1 34.3 %all-gather.5.cloned.1.call-done = bf16[1024,1664]{1,0:T(8,128)(2,1)} async-done(((bf16[32,1664]{1,0:T(8,128)(2,1)}), bf16[1024,1664]{1,0:T(8,128)(2,1)}) %all-gather.5.cloned.1.call-update) | async-done | bytes 3407888 | tf_op jit(solution)/shard_map/all_gather | solution.py:198
  611.3 3.7 fusion.10
  615.1 5.5 multiply_reduce_fusion.1
  620.6 3.5 convolution_add_fusion
  (95 shorter events, 61.0 us)
Async XLA Ops:
  8.0 87.0 %copy-start = (bf16[1024,1664]{1,0:T(8,128)(2,1)S(1)}, bf16[1024,1664]{1,0:T(8,128)(2,1)}, u32[]{:S(2)}) copy-start(bf16[1024,1664]{1,0:T(8,128)(2,1)} %param.8) | copy-start | bytes 10223620
  8.0 152.6 %all-reduce.11.cloned.1.call-start = ((), (), s32[]{:S(2)}) async-start(), calls=%async_computation.2 | async-start | bytes 425984 | tf_op jit(solution)/shard_map/psum | solution.py:109
  8.1 3.1 copy-start.1
  11.2 5.0 copy-start.11
  11.2 5.0 copy-start.5
  17.5 3.9 copy-start.2
  22.9 281.7 %all-reduce.13.cloned.1.call-start = ((), (), s32[]{:S(2)}) async-start(), calls=%async_computation.3 | async-start | bytes 425984 | tf_op jit(solution)/shard_map/psum | solution.py:109
  94.4 0.6 copy-start.9
  96.4 59.7 %copy-start.8 = (f32[2,4,4,4]{3,2,1,0:T(4,128)S(1)}, f32[2,4,4,4]{3,2,1,0:T(4,128)}, u32[]{:S(2)}) copy-start(f32[2,4,4,4]{3,2,1,0:T(4,128)} %param.10) | copy-start | bytes 1540
  148.7 2.9 copy-start.7
  150.4 1.2 copy-start.3
  165.4 7.6 %copy-start.13 = (f32[2,4,4,4]{3,2,1,0:T(4,128)S(1)}, f32[2,4,4,4]{3,2,1,0:T(4,128)}, u32[]{:S(2)}) copy-start(f32[2,4,4,4]{3,2,1,0:T(4,128)} %param.12) | copy-start | bytes 1540
  202.6 368.5 %all-reduce.15.cloned.1.call-start = ((), (), s32[]{:S(2)}) async-start(), calls=%async_computation.5 | async-start | bytes 425984 | tf_op jit(solution)/shard_map/psum | solution.py:183
  204.0 100.6 %copy-start.16 = (f32[32]{0:T(128)S(1)}, f32[32]{0:T(128)}, u32[]{:S(2)}) copy-start(f32[32]{0:T(128)} %get-tuple-element.26) | copy-start | bytes 388
  204.0 103.0 %copy-start.12 = (f32[1024]{0:T(1024)S(1)}, f32[1024]{0:T(1024)}, u32[]{:S(2)}) copy-start(f32[1024]{0:T(1024)} %dynamic-update-slice) | copy-start | bytes 12292
  204.0 235.5 %copy-start.10 = (f32[1024]{0:T(1024)S(1)}, f32[1024]{0:T(1024)}, u32[]{:S(2)}) copy-start(f32[1024]{0:T(1024)} %copy-done.9) | copy-start | bytes 12292
  306.5 0.5 copy-start.18
  445.0 128.9 %all-gather.3.cloned.1.call-start = ((), (), s32[]{:S(2)}) async-start(), calls=%async_computation.1 | async-start | bytes 3514368 | tf_op jit(solution)/shard_map/all_gather | solution.py:199
  445.6 165.8 %all-gather.5.cloned.1.call-start = ((), (), s32[]{:S(2)}) async-start(), calls=%async_computation.4 | async-start | bytes 3514368 | tf_op jit(solution)/shard_map/all_gather | solution.py:198
  449.0 166.0 %all-to-all-start = ((bf16[32,32,1664]{2,1,0:T(8,128)(2,1)}), bf16[32,32,1664]{2,1,0:T(8,128)(2,1)}, u32[]{:S(2)}, u32[]{:S(2)}) async-start(bf16[32,32,1664]{2,1,0:T(8,128)(2,1)} %stack.8), calls=%async_computation | async-start | bytes 6815744 | tf_op jit(solution)/shard_map/all_to_all | solution.py:190
  459.7 5.2 copy-start.4
  460.6 110.4 %copy-start.6 = (bf16[32,1664]{1,0:T(8,128)(2,1)S(1)}, bf16[32,1664]{1,0:T(8,128)(2,1)}, u32[]{:S(2)}) copy-start(bf16[32,1664]{1,0:T(8,128)(2,1)} %param.9) | copy-start | bytes 319492
  460.6 110.4 %copy-start.15 = (f32[32]{0:T(128)S(1)}, f32[32]{0:T(128)}, u32[]{:S(2)}) copy-start(f32[32]{0:T(128)} %copy-done.14) | copy-start | bytes 388
  573.9 41.2 %copy-start.17 = (f32[1024]{0:T(1024)S(1)}, f32[1024]{0:T(1024)}, u32[]{:S(2)}) copy-start(f32[1024]{0:T(1024)} %get-tuple-element.21) | copy-start | bytes 12292
  (1 other events, 0.5 us)
Sparse Core Ops, SparseCore 0:
  23.0 102.7 all-reduce.10
  202.7 101.8 all-reduce.12
  445.1 125.8 all-reduce.14
Sparse Core Ops, SparseCore 1:
  447.3 97.1 all-gather.2
  546.2 65.1 all-gather.4
